TPU v7x, 32 devices: a whole 2x2x4 slice. The times are simulated.
32 devices in a mesh: grp: 4 (over y, x), row: 2 (over core), col: 4 (over z).
Axes of the slice: x: 2, y: 2, z: 4, core: 2. Of those that a mesh axis runs over, the one named last changes fastest.
Arguments:
- normals: float32 [4, 4096, 4096], P('grp', 'row', 'col'), as said below
- transforms: float32 [4, 32, 128, 128], P('grp', 'row'), as said below
- block_map: int32 [4, 32], P('grp'), may hold values from 0 to 31, as said below
Outputs:
- eliminated: float32 [4096, 4096], P('row', 'col')
Inputs may be any that keep to these rules, and one draw needn't show every extreme that they name: `block_map`: for each group, a permutation of the blocks that maps every aligned range of 8 blocks onto itself. `normals`: each group's matrix is symmetric positive definite. `transforms`: each block is nonsingular.
All inputs are finite; a program needn't handle non-finite values.
Results may differ from a plain program's by a relative error of at most 0.0001.
Values sent between devices are 32-bit elements; how exact they have to be, the bound alone decides.
No kernel may reach another device: no remote copies, remote signals or barrier semaphores. Data moves between devices by JAX's collectives and lax.ppermute only.
A program may use at most 64 MiB of HBM per device.

v0:
```python
import jax
import jax.numpy as jnp
from jax import lax
from jax.sharding import PartitionSpec as P

BLK = 128
NPAN = 5


def spread(block, axis, holder):
    block = jnp.where(lax.axis_index(axis) == holder, block, jnp.zeros_like(block))
    return lax.psum(block, axis)


def on_device(normals, transforms, block_map):
    local = normals[0]
    height, width = local.shape
    row_blocks = height // BLK
    col_blocks = width // BLK
    row_index = lax.axis_index("row")
    col_index = lax.axis_index("col")
    row_transforms = transforms[0]
    every_block = lax.all_gather(transforms, "row", axis=1, tiled=True)[0]
    col_transforms = lax.dynamic_slice_in_dim(every_block, col_index * col_blocks, col_blocks, 0)
    grid = local.reshape(row_blocks, BLK, col_blocks, BLK)
    half_done = jnp.einsum("aij,aibk->ajbk", row_transforms, grid, precision=lax.Precision.HIGHEST)
    rotated = jnp.einsum(
        "ajbk,bkl->ajbl", half_done, col_transforms, precision=lax.Precision.HIGHEST
    )
    mapping = block_map[0]
    row_map = (
        lax.dynamic_slice_in_dim(mapping, row_index * row_blocks, row_blocks, 0)
        - row_index * row_blocks
    )
    col_map = (
        lax.dynamic_slice_in_dim(mapping, col_index * col_blocks, col_blocks, 0)
        - col_index * col_blocks
    )
    rotated = jnp.take(rotated, row_map, axis=0)
    rotated = jnp.take(rotated, col_map, axis=2).reshape(height, width)
    matrix = lax.psum(rotated, "grp")
    row_offset = row_index * height
    own_count = matrix.shape[0]
    order_all = height * lax.axis_size("row")
    col_offset = col_index * width
    for panel in range(NPAN):
        offset = panel * BLK
        holder = offset // width
        inside = offset - holder * width
        panel_piece = spread(matrix[:, inside : inside + BLK], "col", holder)
        column = lax.all_gather(panel_piece, "row", axis=0, tiled=True)
        factor_block = jnp.linalg.cholesky(column[offset : offset + BLK])
        factor = lax.linalg.triangular_solve(
            factor_block, column, left_side=False, lower=True, transpose_a=True
        )
        below = jnp.arange(order_all)[:, None] >= offset
        factor = jnp.where(below, factor, jnp.zeros_like(factor))
        own_rows = lax.dynamic_slice_in_dim(factor, row_offset, own_count, 0)
        col_rows = lax.dynamic_slice_in_dim(factor, col_offset, width, 0)
        matrix = matrix - jnp.dot(
            own_rows,
            col_rows.T,
            precision=lax.Precision.HIGHEST,
            preferred_element_type=jnp.float32,
        )
        current = matrix[:, inside : inside + BLK]
        matrix = matrix.at[:, inside : inside + BLK].set(
            jnp.where(col_index == holder, own_rows, current)
        )
    return matrix


def solution(mesh):
    return jax.shard_map(
        on_device,
        mesh=mesh,
        in_specs=(P("grp", "row", "col"), P("grp", "row", None, None), P("grp", None)),
        out_specs=P("row", "col"),
        check_vma=False,
    )
```

profile of v0, /device:TPU:0, one launch (start us, length us, event | category | flops | bytes accessed | tf_op | source)
XLA Modules:
  0.0 811.8 jit_solution(7198959561113941672)
XLA Ops:
  16.7 14.3 %fusion = f32[16,128,8,128]{3,1,0,2:T(8,128)} fusion(f32[16,128,8,128]{3,2,1,0:T(8,128)} %bitcast.108, f32[1,16,128,128]{3,2,1,0:T(8,128)S(1)} %copy-done.4), kind=kOutput, calls=%fused_computation.3 | convolution fusion | flops 3221225472 | bytes 17825792 | tf_op jit(solution)/shard_map/aij,aibk->ajbk/dot_general | solution.py:26
  31.0 12.0 %convolution_bitcast_fusion.5 = f32[16,128,8,128]{1,3,0,2:T(8,128)} fusion(f32[16,128,8,128]{3,1,0,2:T(8,128)} %fusion, f32[1,32,128,128]{3,2,0,1:T(8,128)} %all-gather.7.cloned.1.call-done, s32[]{:T(128)S(6)} %select_n.123), kind=kOutput, calls=%fused_computation.20 | convolution fusion | flops 3221225472 | bytes 17301508 | tf_op jit(solution)/shard_map/ajbk,bkl->ajbl/dot_general | solution.py:27
  82.2 174.8 %all-reduce.7.cloned.1.call-done = f32[2048,1024]{0,1:T(8,128)} async-done(((f32[2048,1024]{0,1:T(8,128)}), f32[2048,1024]{0,1:T(8,128)}) %all-reduce.7.cloned.1.call-update) | async-done | bytes 8388624 | tf_op jit(solution)/shard_map/psum | solution.py:41
  259.4 52.7 %all-reduce.9.cloned.1.call-done = f32[2048,128]{0,1:T(8,128)} async-done(((f32[2048,128]{0,1:T(8,128)}), f32[2048,128]{0,1:T(8,128)}) %all-reduce.9.cloned.1.call-update) | async-done | bytes 1048592 | tf_op jit(solution)/shard_map/psum | solution.py:12
  313.0 10.3 %all-gather.9.cloned.1.call-done = f32[4096,128]{0,1:T(8,128)} async-done(((f32[2048,128]{0,1:T(8,128)}), f32[4096,128]{0,1:T(8,128)}) %all-gather.9.cloned.1.call-update) | async-done | bytes 2097168 | tf_op jit(solution)/shard_map/all_gather | solution.py:51
  325.1 11.7 %cholesky.89 = f32[128,128]{1,0:T(8,128)S(1)} custom-call(f32[128,128]{1,0:T(8,128)S(1)} %fusion.38), custom_call_target="Cholesky" | custom-call | tf_op jit(solution)/shard_map/jit(cholesky)/cholesky | solution.py:52
  338.2 9.8 %custom-call.9 = f32[1,128,128]{1,2,0:T(8,128)S(1)} custom-call(f32[1,128,128]{2,1,0:T(8,128)S(1)} %fusion.24), custom_call_target="InvertDiagBlocksLowerTriangular" | custom-call | tf_op jit(solution)/shard_map/triangular_solve/custom-call.0 | solution.py:53
  366.4 53.2 %all-reduce.11.cloned.1.call-done = f32[2048,128]{0,1:T(8,128)} async-done(((f32[2048,128]{0,1:T(8,128)}), f32[2048,128]{0,1:T(8,128)}) %all-reduce.11.cloned.1.call-update) | async-done | bytes 1048592 | tf_op jit(solution)/shard_map/psum | solution.py:12
  420.7 10.1 %all-gather.11.cloned.1.call-done = f32[4096,128]{0,1:T(8,128)} async-done(((f32[2048,128]{0,1:T(8,128)}), f32[4096,128]{0,1:T(8,128)}) %all-gather.11.cloned.1.call-update) | async-done | bytes 2097168 | tf_op jit(solution)/shard_map/all_gather | solution.py:51
  432.6 11.7 %cholesky.100 = f32[128,128]{1,0:T(8,128)S(1)} custom-call(f32[128,128]{1,0:T(8,128)S(1)} %fusion.36), custom_call_target="Cholesky" | custom-call | tf_op jit(solution)/shard_map/jit(cholesky)/cholesky | solution.py:52
  445.7 9.8 %custom-call.10 = f32[1,128,128]{1,2,0:T(8,128)S(1)} custom-call(f32[1,128,128]{2,1,0:T(8,128)S(1)} %fusion.25), custom_call_target="InvertDiagBlocksLowerTriangular" | custom-call | tf_op jit(solution)/shard_map/triangular_solve/custom-call.0 | solution.py:53
  473.8 53.2 %all-reduce.13.cloned.1.call-done = f32[2048,128]{0,1:T(8,128)} async-done(((f32[2048,128]{0,1:T(8,128)}), f32[2048,128]{0,1:T(8,128)}) %all-reduce.13.cloned.1.call-update) | async-done | bytes 1048592 | tf_op jit(solution)/shard_map/psum | solution.py:12
  527.9 10.6 %all-gather.13.cloned.1.call-done = f32[4096,128]{0,1:T(8,128)} async-done(((f32[2048,128]{0,1:T(8,128)}), f32[4096,128]{0,1:T(8,128)}) %all-gather.13.cloned.1.call-update) | async-done | bytes 2097168 | tf_op jit(solution)/shard_map/all_gather | solution.py:51
  540.2 11.7 %cholesky.111 = f32[128,128]{1,0:T(8,128)S(1)} custom-call(f32[128,128]{1,0:T(8,128)S(1)} %fusion.34), custom_call_target="Cholesky" | custom-call | tf_op jit(solution)/shard_map/jit(cholesky)/cholesky | solution.py:52
  553.2 9.8 %custom-call.11 = f32[1,128,128]{1,2,0:T(8,128)S(1)} custom-call(f32[1,128,128]{2,1,0:T(8,128)S(1)} %fusion.26), custom_call_target="InvertDiagBlocksLowerTriangular" | custom-call | tf_op jit(solution)/shard_map/triangular_solve/custom-call.0 | solution.py:53
  581.8 52.8 %all-reduce.15.cloned.1.call-done = f32[2048,128]{0,1:T(8,128)} async-done(((f32[2048,128]{0,1:T(8,128)}), f32[2048,128]{0,1:T(8,128)}) %all-reduce.15.cloned.1.call-update) | async-done | bytes 1048592 | tf_op jit(solution)/shard_map/psum | solution.py:12
  635.3 10.6 %all-gather.15.cloned.1.call-done = f32[4096,128]{0,1:T(8,128)} async-done(((f32[2048,128]{0,1:T(8,128)}), f32[4096,128]{0,1:T(8,128)}) %all-gather.15.cloned.1.call-update) | async-done | bytes 2097168 | tf_op jit(solution)/shard_map/all_gather | solution.py:51
  647.6 11.7 %cholesky.122 = f32[128,128]{1,0:T(8,128)S(1)} custom-call(f32[128,128]{1,0:T(8,128)S(1)} %fusion.32), custom_call_target="Cholesky" | custom-call | tf_op jit(solution)/shard_map/jit(cholesky)/cholesky | solution.py:52
  660.7 9.8 %custom-call.12 = f32[1,128,128]{1,2,0:T(8,128)S(1)} custom-call(f32[1,128,128]{2,1,0:T(8,128)S(1)} %fusion.27), custom_call_target="InvertDiagBlocksLowerTriangular" | custom-call | tf_op jit(solution)/shard_map/triangular_solve/custom-call.0 | solution.py:53
  689.0 53.0 %all-reduce.17.cloned.1.call-done = f32[2048,128]{0,1:T(8,128)} async-done(((f32[2048,128]{0,1:T(8,128)}), f32[2048,128]{0,1:T(8,128)}) %all-reduce.17.cloned.1.call-update) | async-done | bytes 1048592 | tf_op jit(solution)/shard_map/psum | solution.py:12
  742.7 10.6 %all-gather.17.cloned.1.call-done = f32[4096,128]{0,1:T(8,128)} async-done(((f32[2048,128]{0,1:T(8,128)}), f32[4096,128]{0,1:T(8,128)}) %all-gather.17.cloned.1.call-update) | async-done | bytes 2097168 | tf_op jit(solution)/shard_map/all_gather | solution.py:51
  755.1 11.7 %cholesky.133 = f32[128,128]{1,0:T(8,128)S(1)} custom-call(f32[128,128]{1,0:T(8,128)S(1)} %fusion.30), custom_call_target="Cholesky" | custom-call | tf_op jit(solution)/shard_map/jit(cholesky)/cholesky | solution.py:52
  768.1 9.8 %custom-call.13 = f32[1,128,128]{1,2,0:T(8,128)S(1)} custom-call(f32[1,128,128]{2,1,0:T(8,128)S(1)} %fusion.28), custom_call_target="InvertDiagBlocksLowerTriangular" | custom-call | tf_op jit(solution)/shard_map/triangular_solve/custom-call.0 | solution.py:53
  781.5 11.2 %convolution_subtract_fusion = f32[2048,1024]{0,1:T(8,128)} fusion(f32[2048,1024]{0,1:T(8,128)} %copy-done.3, f32[4096,128]{0,1:T(8,128)S(1)} %fusion.2, s32[]{:T(128)S(6)} %select_n.133, s32[]{:T(128)S(6)} %select_n.134), kind=kOutput, calls=%fused_computation.14 | convolution fusion | flops 3223322624 | bytes 18350088 | tf_op jit(solution)/shard_map/dot_general | solution.py:60
  (109 shorter events, 160.8 us)
Async XLA Ops:
  6.5 24.5 %all-gather.7.cloned.1.call-start = ((), (), s32[]{:S(2)}) async-start(), calls=%async_computation | async-start | bytes 3145728 | tf_op jit(solution)/shard_map/all_gather | solution.py:23
  7.3 249.7 %all-reduce.7.cloned.1.call-start = ((), (), s32[]{:S(2)}) async-start(), calls=%async_computation.1 | async-start | bytes 16777216 | tf_op jit(solution)/shard_map/psum | solution.py:41
  7.3 9.0 %copy-start.5 = (s32[1,32]{1,0:T(1,128)S(1)}, s32[1,32]{1,0:T(1,128)}, u32[]{:S(2)}) copy-start(s32[1,32]{1,0:T(1,128)} %param.18) | copy-start | bytes 388
  7.3 9.4 %copy-start.4 = (f32[1,16,128,128]{3,2,1,0:T(8,128)S(1)}, f32[1,16,128,128]{3,2,1,0:T(8,128)}, u32[]{:S(2)}) copy-start(f32[1,16,128,128]{3,2,1,0:T(8,128)} %param.17) | copy-start | bytes 3145732
  82.1 229.9 %all-reduce.9.cloned.1.call-start = ((), (), s32[]{:S(2)}) async-start(), calls=%async_computation.2 | async-start | bytes 2097152 | tf_op jit(solution)/shard_map/psum | solution.py:12
  259.3 64.0 %all-gather.9.cloned.1.call-start = ((), (), s32[]{:S(2)}) async-start(), calls=%async_computation.3 | async-start | bytes 3145728 | tf_op jit(solution)/shard_map/all_gather | solution.py:51
  312.1 107.5 %all-reduce.11.cloned.1.call-start = ((), (), s32[]{:S(2)}) async-start(), calls=%async_computation.4 | async-start | bytes 2097152 | tf_op jit(solution)/shard_map/psum | solution.py:12
  361.8 3.4 copy-start
  366.3 64.5 %all-gather.11.cloned.1.call-start = ((), (), s32[]{:S(2)}) async-start(), calls=%async_computation.5 | async-start | bytes 3145728 | tf_op jit(solution)/shard_map/all_gather | solution.py:51
  419.6 107.4 %all-reduce.13.cloned.1.call-start = ((), (), s32[]{:S(2)}) async-start(), calls=%async_computation.6 | async-start | bytes 2097152 | tf_op jit(solution)/shard_map/psum | solution.py:12
  469.3 3.4 copy-start.1
  473.8 64.6 %all-gather.13.cloned.1.call-start = ((), (), s32[]{:S(2)}) async-start(), calls=%async_computation.7 | async-start | bytes 3145728 | tf_op jit(solution)/shard_map/all_gather | solution.py:51
  527.0 107.6 %all-reduce.15.cloned.1.call-start = ((), (), s32[]{:S(2)}) async-start(), calls=%async_computation.8 | async-start | bytes 2097152 | tf_op jit(solution)/shard_map/psum | solution.py:12
  576.9 3.4 copy-start.2
  581.3 64.5 %all-gather.15.cloned.1.call-start = ((), (), s32[]{:S(2)}) async-start(), calls=%async_computation.9 | async-start | bytes 3145728 | tf_op jit(solution)/shard_map/all_gather | solution.py:51
  634.6 107.4 %all-reduce.17.cloned.1.call-start = ((), (), s32[]{:S(2)}) async-start(), calls=%async_computation.10 | async-start | bytes 2097152 | tf_op jit(solution)/shard_map/psum | solution.py:12
  684.3 3.4 copy-start.3
  688.8 64.5 %all-gather.17.cloned.1.call-start = ((), (), s32[]{:S(2)}) async-start(), calls=%async_computation.11 | async-start | bytes 3145728 | tf_op jit(solution)/shard_map/all_gather | solution.py:51
Sparse Core Ops, SparseCore 0:
  8.9 13.3 all-gather.6
  82.2 174.7 all-reduce.6
  259.4 52.5 all-reduce.8
  313.4 9.8 all-gather.8
  366.5 53.0 all-reduce.10
  421.0 9.8 all-gather.10
  473.9 53.0 all-reduce.12
  528.5 9.8 all-gather.12
  581.5 53.0 all-reduce.14
  636.0 9.8 all-gather.14
  688.9 53.0 all-reduce.16
  743.4 9.8 all-gather.16
where the time goes:
time: 821 us; the launch traced here: 812 us
  waiting for transfers between devices  493 us (60%)
  other arithmetic  151 us (18%)
  matrix products  92.7 us (11%)
  local copies, waits for them, and re-layouts  60 us (7%)
  between operations  14.1 us (2%)
    psum x5, waiting for transfers between devices, spread(): return lax.psum(block, axis)  265 us
    psum x1, waiting for transfers between devices, on_device(): matrix = lax.psum(rotated, 'grp')  175 us
    another operation x15, other arithmetic, on_device(): factor_block = jnp.linalg.cholesky(column[offset:offset + BLK])  62 us
    another operation x10, other arithmetic, on_device(): lax.linalg.triangular_solve(factor_block, column, left_side=False, lower=...  52.2 us
    all_gather x5, waiting for transfers between devices, on_device(): column = lax.all_gather(panel_piece, 'row', axis=0, tiled=True)  52.2 us
    dot_general x5, matrix products, on_device(): jnp.dot(own_rows, col_rows.T, precision=lax.Precision.HIGHEST, preferred_...  48.8 us
    unnamed x13, local copies, waits for them, and re-layouts  22.5 us
    another operation x5, matrix products, on_device(): lax.linalg.triangular_solve(factor_block, column, left_side=False, lower=...  17.5 us
  transfers between devices with their start and end apart: 12, of which 11 were waited for; matrix products, arithmetic and copies ran while one was open for 3% of the time, Pallas kernels for 0%

commit v1 on v0

--- a/solution.py
+++ b/solution.py
@@ -9,7 +9,7 @@
 
 def spread(block, axis, holder):
     block = jnp.where(lax.axis_index(axis) == holder, block, jnp.zeros_like(block))
-    return lax.psum(block, axis)
+    return jnp.sum(lax.all_gather(block, axis_name=axis), axis=0)
 
 
 def on_device(normals, transforms, block_map):

time: 821 us -> 1020 us (1.24)
  waiting for transfers between devices: 493 us -> 627 us
  local copies, waits for them, and re-layouts: 60 us -> 90.1 us
  other arithmetic: 151 us -> 180 us
    all_gather x0 -> x5, waiting for transfers between devices: none -> 409 us  [spread(): return jnp.sum(lax.all_gather(block, axis_name=axis), axis=0)]
    psum x5 -> x0, waiting for transfers between devices: 265 us -> none  [spread(): return lax.psum(block, axis)]
    all_gather x0 -> x5, local copies, waits for them, and re-layouts: none -> 30.1 us  [spread(): return jnp.sum(lax.all_gather(block, axis_name=axis), axis=0)]
    reduce_sum x0 -> x5, other arithmetic: none -> 29.1 us  [spread(): return jnp.sum(lax.all_gather(block, axis_name=axis), axis=0)]
where the time goes in v1:
time: 1020 us; the launch traced here: 1010 us
  waiting for transfers between devices  627 us (61%)
  other arithmetic  180 us (18%)
  matrix products  92.9 us (9%)
  local copies, waits for them, and re-layouts  90.1 us (9%)
  between operations  14.4 us (1%)
    all_gather x5, waiting for transfers between devices, spread(): return jnp.sum(lax.all_gather(block, axis_name=axis), axis=0)  409 us
    psum x1, waiting for transfers between devices, on_device(): matrix = lax.psum(rotated, 'grp')  175 us
    another operation x15, other arithmetic, on_device(): factor_block = jnp.linalg.cholesky(column[offset:offset + BLK])  62 us
    another operation x10, other arithmetic, on_device(): lax.linalg.triangular_solve(factor_block, column, left_side=False, lower=...  52.2 us
    dot_general x5, matrix products, on_device(): jnp.dot(own_rows, col_rows.T, precision=lax.Precision.HIGHEST, preferred_...  49.1 us
    all_gather x5, waiting for transfers between devices, on_device(): column = lax.all_gather(panel_piece, 'row', axis=0, tiled=True)  42.3 us
    all_gather x5, local copies, waits for them, and re-layouts, spread(): return jnp.sum(lax.all_gather(block, axis_name=axis), axis=0)  30.1 us
    reduce_sum x5, other arithmetic, spread(): return jnp.sum(lax.all_gather(block, axis_name=axis), axis=0)  29.1 us
  transfers between devices with their start and end apart: 12, of which 11 were waited for; matrix products, arithmetic and copies ran while one was open for 3% of the time, Pallas kernels for 0%

profile of v1, /device:TPU:0, one launch (start us, length us, event | category | flops | bytes accessed | tf_op | source)
XLA Modules:
  0.0 1005.4 jit_solution(16461352752981952374)
XLA Ops:
  16.7 14.3 %fusion = f32[16,128,8,128]{3,1,0,2:T(8,128)} fusion(f32[16,128,8,128]{3,2,1,0:T(8,128)} %bitcast.119, f32[1,16,128,128]{3,2,1,0:T(8,128)S(1)} %copy-done.4), kind=kOutput, calls=%fused_computation.3 | convolution fusion | flops 3221225472 | bytes 17825792 | tf_op jit(solution)/shard_map/aij,aibk->ajbk/dot_general | solution.py:26
  31.0 12.0 %convolution_bitcast_fusion.5 = f32[16,128,8,128]{1,3,0,2:T(8,128)} fusion(f32[16,128,8,128]{3,1,0,2:T(8,128)} %fusion, f32[1,32,128,128]{3,2,0,1:T(8,128)} %all-gather.17.cloned.1.call-done, s32[]{:T(128)S(6)} %select_n.123), kind=kOutput, calls=%fused_computation.20 | convolution fusion | flops 3221225472 | bytes 17301508 | tf_op jit(solution)/shard_map/ajbk,bkl->ajbl/dot_general | solution.py:27
  82.2 174.8 %all-reduce.2.cloned.1.call-done = f32[2048,1024]{0,1:T(8,128)} async-done(((f32[2048,1024]{0,1:T(8,128)}), f32[2048,1024]{0,1:T(8,128)}) %all-reduce.2.cloned.1.call-update) | async-done | bytes 8388624 | tf_op jit(solution)/shard_map/psum | solution.py:41
  259.4 81.5 %all-gather.29.cloned.1.call-done = f32[8192,128]{0,1:T(8,128)} async-done(((f32[2048,128]{0,1:T(8,128)}), f32[8192,128]{0,1:T(8,128)}) %all-gather.29.cloned.1.call-update) | async-done | bytes 4194320 | tf_op jit(solution)/shard_map/all_gather | solution.py:12
  363.8 11.7 %cholesky.89 = f32[128,128]{1,0:T(8,128)S(1)} custom-call(f32[128,128]{1,0:T(8,128)S(1)} %fusion.38), custom_call_target="Cholesky" | custom-call | tf_op jit(solution)/shard_map/jit(cholesky)/cholesky | solution.py:52
  376.8 9.8 custom-call.9
  390.2 9.4 convolution_subtract_fusion.4
  405.2 81.8 %all-gather.31.cloned.1.call-done = f32[8192,128]{0,1:T(8,128)} async-done(((f32[2048,128]{0,1:T(8,128)}), f32[8192,128]{0,1:T(8,128)}) %all-gather.31.cloned.1.call-update) | async-done | bytes 4194320 | tf_op jit(solution)/shard_map/all_gather | solution.py:12
  509.9 11.7 %cholesky.100 = f32[128,128]{1,0:T(8,128)S(1)} custom-call(f32[128,128]{1,0:T(8,128)S(1)} %fusion.36), custom_call_target="Cholesky" | custom-call | tf_op jit(solution)/shard_map/jit(cholesky)/cholesky | solution.py:52
  523.0 9.8 custom-call.10
  536.3 9.4 convolution_subtract_fusion.3
  551.5 81.6 %all-gather.33.cloned.1.call-done = f32[8192,128]{0,1:T(8,128)} async-done(((f32[2048,128]{0,1:T(8,128)}), f32[8192,128]{0,1:T(8,128)}) %all-gather.33.cloned.1.call-update) | async-done | bytes 4194320 | tf_op jit(solution)/shard_map/all_gather | solution.py:12
  656.0 11.7 %cholesky.111 = f32[128,128]{1,0:T(8,128)S(1)} custom-call(f32[128,128]{1,0:T(8,128)S(1)} %fusion.34), custom_call_target="Cholesky" | custom-call | tf_op jit(solution)/shard_map/jit(cholesky)/cholesky | solution.py:52
  669.0 9.8 custom-call.11
  682.4 9.4 convolution_subtract_fusion.2
  697.4 81.8 %all-gather.35.cloned.1.call-done = f32[8192,128]{0,1:T(8,128)} async-done(((f32[2048,128]{0,1:T(8,128)}), f32[8192,128]{0,1:T(8,128)}) %all-gather.35.cloned.1.call-update) | async-done | bytes 4194320 | tf_op jit(solution)/shard_map/all_gather | solution.py:12
  802.1 11.7 %cholesky.122 = f32[128,128]{1,0:T(8,128)S(1)} custom-call(f32[128,128]{1,0:T(8,128)S(1)} %fusion.32), custom_call_target="Cholesky" | custom-call | tf_op jit(solution)/shard_map/jit(cholesky)/cholesky | solution.py:52
  815.1 9.8 custom-call.12
  828.4 9.4 convolution_subtract_fusion.1
  843.5 81.8 %all-gather.37.cloned.1.call-done = f32[8192,128]{0,1:T(8,128)} async-done(((f32[2048,128]{0,1:T(8,128)}), f32[8192,128]{0,1:T(8,128)}) %all-gather.37.cloned.1.call-update) | async-done | bytes 4194320 | tf_op jit(solution)/shard_map/all_gather | solution.py:12
  948.2 11.7 %cholesky.133 = f32[128,128]{1,0:T(8,128)S(1)} custom-call(f32[128,128]{1,0:T(8,128)S(1)} %fusion.30), custom_call_target="Cholesky" | custom-call | tf_op jit(solution)/shard_map/jit(cholesky)/cholesky | solution.py:52
  961.2 9.8 custom-call.13
  974.5 11.4 %convolution_subtract_fusion = f32[2048,1024]{0,1:T(8,128)} fusion(f32[2048,1024]{0,1:T(8,128)} %copy-done.3, f32[4096,128]{0,1:T(8,128)S(1)} %fusion.2, s32[]{:T(128)S(6)} %select_n.133, s32[]{:T(128)S(6)} %select_n.134), kind=kOutput, calls=%fused_computation.14 | convolution fusion | flops 3223322624 | bytes 18350088 | tf_op jit(solution)/shard_map/dot_general | solution.py:60
  988.9 9.2 copy.46
  (119 shorter events, 215.3 us)
Async XLA Ops:
  6.5 24.5 %all-gather.17.cloned.1.call-start = ((), (), s32[]{:S(2)}) async-start(), calls=%async_computation | async-start | bytes 3145728 | tf_op jit(solution)/shard_map/all_gather | solution.py:23
  7.3 249.8 %all-reduce.2.cloned.1.call-start = ((), (), s32[]{:S(2)}) async-start(), calls=%async_computation.1 | async-start | bytes 16777216 | tf_op jit(solution)/shard_map/psum | solution.py:41
  7.3 9.0 copy-start.5
  7.3 9.4 copy-start.4
  82.1 258.8 %all-gather.29.cloned.1.call-start = ((), (), s32[]{:S(2)}) async-start(), calls=%async_computation.7 | async-start | bytes 5242880 | tf_op jit(solution)/shard_map/all_gather | solution.py:12
  259.3 102.7 %all-gather.19.cloned.1.call-start = ((), (), s32[]{:S(2)}) async-start(), calls=%async_computation.2 | async-start | bytes 3145728 | tf_op jit(solution)/shard_map/all_gather | solution.py:51
  352.8 134.3 %all-gather.31.cloned.1.call-start = ((), (), s32[]{:S(2)}) async-start(), calls=%async_computation.8 | async-start | bytes 5242880 | tf_op jit(solution)/shard_map/all_gather | solution.py:12
  400.5 3.4 copy-start
  405.0 103.1 %all-gather.21.cloned.1.call-start = ((), (), s32[]{:S(2)}) async-start(), calls=%async_computation.3 | async-start | bytes 3145728 | tf_op jit(solution)/shard_map/all_gather | solution.py:51
  498.9 134.2 %all-gather.33.cloned.1.call-start = ((), (), s32[]{:S(2)}) async-start(), calls=%async_computation.9 | async-start | bytes 5242880 | tf_op jit(solution)/shard_map/all_gather | solution.py:12
  546.6 3.4 copy-start.1
  551.1 103.2 %all-gather.23.cloned.1.call-start = ((), (), s32[]{:S(2)}) async-start(), calls=%async_computation.4 | async-start | bytes 3145728 | tf_op jit(solution)/shard_map/all_gather | solution.py:51
  645.0 134.2 %all-gather.35.cloned.1.call-start = ((), (), s32[]{:S(2)}) async-start(), calls=%async_computation.10 | async-start | bytes 5242880 | tf_op jit(solution)/shard_map/all_gather | solution.py:12
  692.7 3.4 copy-start.2
  697.1 103.1 %all-gather.25.cloned.1.call-start = ((), (), s32[]{:S(2)}) async-start(), calls=%async_computation.5 | async-start | bytes 3145728 | tf_op jit(solution)/shard_map/all_gather | solution.py:51
  791.1 134.2 %all-gather.37.cloned.1.call-start = ((), (), s32[]{:S(2)}) async-start(), calls=%async_computation.11 | async-start | bytes 5242880 | tf_op jit(solution)/shard_map/all_gather | solution.py:12
  838.7 3.4 copy-start.3
  843.2 103.2 %all-gather.27.cloned.1.call-start = ((), (), s32[]{:S(2)}) async-start(), calls=%async_computation.6 | async-start | bytes 3145728 | tf_op jit(solution)/shard_map/all_gather | solution.py:51
Sparse Core Ops, SparseCore 0:
  8.9 13.3 all-gather.16
  82.3 174.7 all-reduce.1
  259.4 81.4 all-gather.28
  352.9 9.0 all-gather.18
  405.1 81.8 all-gather.30
  499.0 9.0 all-gather.20
  551.2 81.9 all-gather.32
  645.1 9.0 all-gather.22
  697.3 81.8 all-gather.34
  791.2 9.0 all-gather.24
  843.3 81.8 all-gather.36
  937.3 9.0 all-gather.26
